TPU v7x, 512 devices: a whole 4x4x16 slice. The times are simulated.
512 devices in a mesh: row: 16 (over z), col: 8 (over x_lo, y), depth: 4 (over x_hi, core).
Axes of the slice: x: 4 (x_hi: 2, x_lo: 2; x = x_hi * 2 + x_lo), y: 4, z: 16, core: 2. Of those that a mesh axis runs over, the one named last changes fastest.
Arguments:
- h_blocks: bfloat16 [16, 16, 4, 12, 128, 128], P('row', 'col', 'depth'), may hold values from -0.25 to 0.25
- h_rows: int32 [16, 16, 4, 12], P('row', 'col', 'depth'), may hold values from 0 to 31, as said below
- h_cols: int32 [16, 16, 4, 12], P('row', 'col', 'depth'), may hold values from 0 to 7
- h_flags: int32 [16, 16, 4, 12], P('row', 'col', 'depth'), may hold values from 0 to 1
- x_blocks: bfloat16 [16, 4, 8, 8, 2, 128, 128], P('row', 'depth', 'col'), may hold values from -6 to 6
- x_cols: int32 [16, 4, 8, 8, 2], P('row', 'depth', 'col'), may hold values from 0 to 7, as said below
- x_flags: int32 [16, 4, 8, 8, 2], P('row', 'depth', 'col'), may hold values from 0 to 1
- previous: bfloat16 [16, 4, 8, 8, 2, 128, 128], P('row', 'depth', 'col'), may hold values from -6 to 6
Outputs:
- next_term: bfloat16 [16, 4, 8, 8, 2, 128, 128], P('row', 'depth', 'col')
Inputs may be any that keep to these rules, and one draw needn't show every extreme that they name: The slots of one tile (g, p, e) name distinct positions (h_rows, h_cols); live slots come first; every tile with g = p has all 12 slots live. `x_cols`: the 2 slots of one block row in one column group name distinct columns.
All inputs are finite; a program needn't handle non-finite values.
Results may differ from a plain program's by a relative error of at most 0.0095.
Values may be sent and summed in bfloat16 or wider, within the bound.
No kernel may reach another device: no remote copies, remote signals or barrier semaphores. Data moves between devices by JAX's collectives and lax.ppermute only.
A program may use at most 64 MiB of HBM per device.

v0:
```python
import jax
import jax.numpy as jnp
from jax import lax
from jax.sharding import PartitionSpec as P


def add_piece(summed, ham_part, iter_part, aim_cols, aim_flags):
    blocks, ham_rows, ham_cols, ham_flags = ham_part
    iter_blocks, iter_cols, iter_flags = iter_part
    iter_width = iter_cols.shape[-1]
    picked = jnp.take(iter_blocks, ham_cols, axis=0)
    picked_cols = jnp.take(iter_cols, ham_cols, axis=0)
    picked_flags = jnp.take(iter_flags, ham_cols, axis=0)
    wanted_cols = jnp.take(aim_cols, ham_rows, axis=0)
    wanted_flags = jnp.take(aim_flags, ham_rows, axis=0)
    paired = picked_cols[:, :, None] == wanted_cols[:, None, :]
    paired = paired & (picked_flags[:, :, None] > 0) & (wanted_flags[:, None, :] > 0)
    paired = paired & (ham_flags[:, None, None] > 0)
    chosen = jnp.einsum(
        "awv,awkm->avkm", paired.astype(jnp.bfloat16), picked, preferred_element_type=jnp.float32
    ).astype(jnp.bfloat16)
    products = jnp.einsum("akl,avlm->avkm", blocks, chosen, preferred_element_type=jnp.float32)
    target = ham_rows[:, None] * iter_width + jnp.arange(iter_width, dtype=jnp.int32)[None, :]
    return summed.at[target.reshape(-1)].add(products.reshape((-1,) + products.shape[2:]))


def run_pieces(summed, ham_part, iter_part, aim_cols, aim_flags):

    def one_piece(running, element):
        ham_item, iter_item = element
        running = add_piece(running, ham_item, iter_item, aim_cols, aim_flags)
        return (running, None)

    summed, _ = lax.scan(one_piece, summed, (ham_part, iter_part))
    return summed


def body(h_blocks, h_rows, h_cols, h_flags, x_blocks, x_cols, x_flags, previous):
    aim_cols, aim_flags = (
        lax.all_gather(x_cols, "depth", axis=1, tiled=True),
        lax.all_gather(x_flags, "depth", axis=1, tiled=True),
    )
    iter_width = x_cols.shape[-1]
    piece_rows = x_cols.shape[3]
    block_size = x_blocks.shape[-1]
    aim_cols = aim_cols.reshape(-1, iter_width)
    aim_flags = aim_flags.reshape(-1, iter_width)
    group_rows = aim_cols.shape[0]
    summed = jnp.zeros((group_rows * iter_width, block_size, block_size), jnp.float32)
    ham_all = (
        lax.all_gather(h_blocks, "col", axis=1, tiled=True),
        lax.all_gather(h_rows, "col", axis=1, tiled=True),
        lax.all_gather(h_cols, "col", axis=1, tiled=True),
        lax.all_gather(h_flags, "col", axis=1, tiled=True),
    )
    ham_all = tuple((member[0, :, 0] for member in ham_all))
    pieces = (
        lax.all_gather(x_blocks, "row", axis=0, tiled=True),
        lax.all_gather(x_cols, "row", axis=0, tiled=True),
        lax.all_gather(x_flags, "row", axis=0, tiled=True),
    )
    ham_part = tuple((member for member in ham_all))
    iter_part = tuple((member[:, 0, 0] for member in pieces))
    summed = run_pieces(summed, ham_part, iter_part, aim_cols, aim_flags)
    rounded = lax.optimization_barrier(summed.astype(jnp.bfloat16)).astype(jnp.float32)
    rounded = rounded.reshape(
        (lax.axis_size("depth"), piece_rows, iter_width, block_size, block_size)
    )
    shares = lax.psum_scatter(
        rounded.astype(jnp.bfloat16), "depth", scatter_dimension=0, tiled=True
    ).astype(jnp.float32)
    prior = previous[0, 0, 0].astype(jnp.float32)
    live = x_flags[0, 0, 0].astype(jnp.float32)[..., None, None]
    result = (2.0 * shares[0] - prior) * live
    return result.astype(jnp.bfloat16).reshape(previous.shape)


def solution(mesh):
    placed = (
        P("row", "col", "depth", None, None, None),
        P("row", "col", "depth", None),
        P("row", "col", "depth", None),
        P("row", "col", "depth", None),
        P("row", "depth", "col", None, None, None, None),
        P("row", "depth", "col", None, None),
        P("row", "depth", "col", None, None),
        P("row", "depth", "col", None, None, None, None),
    )
    return jax.shard_map(
        body,
        mesh=mesh,
        in_specs=placed,
        out_specs=P("row", "depth", "col", None, None, None, None),
        check_vma=False,
    )
```

profile of v0, /device:TPU:1, one launch (start us, length us, event | category | flops | bytes accessed | tf_op | source)
XLA Modules:
  0.0 491.7 jit_solution(9868348673197642162)
XLA Ops:
  8.1 13.5 %all_gather.30 = s32[1,4,1,8,2]{3,4,2,0,1:T(2,128)S(1)} all-gather(s32[1,1,1,8,2]{3,4,2,0,1:T(2,128)} %bitcast.95), channel_id=1, replica_groups=mesh['row'=16,'col'=8,'depth'=4] {'depth'}, dimensions={1}, use_global_device_ids=true | all-gather | bytes 320 | tf_op jit(solution)/shard_map/all_gather | solution.py:40
  21.6 6.8 %all_gather.32 = s32[1,4,1,8,2]{3,4,2,0,1:T(2,128)S(1)} all-gather(s32[1,1,1,8,2]{3,4,2,0,1:T(2,128)} %bitcast.93), channel_id=1, replica_groups=mesh['row'=16,'col'=8,'depth'=4] {'depth'}, dimensions={1}, use_global_device_ids=true | all-gather | bytes 320 | tf_op jit(solution)/shard_map/all_gather | solution.py:41
  28.5 12.7 %all_gather.27 = s32[1,16,1,12]{3,2,0,1:T(1,128)S(1)} all-gather(s32[1,2,1,12]{3,2,0,1:T(1,128)} %bitcast.96), channel_id=1, replica_groups=mesh['row'=16,'col'=8,'depth'=4] {'col'}, dimensions={1}, use_global_device_ids=true | all-gather | bytes 864 | tf_op jit(solution)/shard_map/all_gather | solution.py:52
  41.2 15.2 %all_gather.29 = s32[1,16,1,12]{3,2,0,1:T(1,128)S(1)} all-gather(s32[1,2,1,12]{3,2,0,1:T(1,128)} %bitcast.97), channel_id=1, replica_groups=mesh['row'=16,'col'=8,'depth'=4] {'col'}, dimensions={1}, use_global_device_ids=true | all-gather | bytes 864 | tf_op jit(solution)/shard_map/all_gather | solution.py:53
  56.4 13.5 %all_gather.33 = s32[1,16,1,12]{3,2,0,1:T(1,128)S(1)} all-gather(s32[1,2,1,12]{3,2,0,1:T(1,128)} %bitcast.98), channel_id=1, replica_groups=mesh['row'=16,'col'=8,'depth'=4] {'col'}, dimensions={1}, use_global_device_ids=true | all-gather | bytes 864 | tf_op jit(solution)/shard_map/all_gather | solution.py:54
  70.0 29.6 %all_gather.28 = s32[16,1,1,8,2]{3,4,2,1,0:T(2,128)S(1)} all-gather(s32[1,1,1,8,2]{3,4,2,1,0:T(2,128)} %param.19), channel_id=1, replica_groups=mesh['row'=16,'col'=8,'depth'=4] {'row'}, dimensions={0}, use_global_device_ids=true | all-gather | bytes 1088 | tf_op jit(solution)/shard_map/all_gather | solution.py:59
  99.5 20.1 %all_gather.31 = s32[16,1,1,8,2]{3,4,2,1,0:T(2,128)S(1)} all-gather(s32[1,1,1,8,2]{3,4,2,1,0:T(2,128)} %param.20), channel_id=1, replica_groups=mesh['row'=16,'col'=8,'depth'=4] {'row'}, dimensions={0}, use_global_device_ids=true | all-gather | bytes 1088 | tf_op jit(solution)/shard_map/all_gather | solution.py:60
  119.6 82.3 %all-gather.3.cloned.1.call-done = bf16[16,1,1,8,2,128,128]{6,5,4,3,2,1,0:T(8,128)(2,1)} async-done(((bf16[1,1,1,8,2,128,128]{6,5,4,3,2,1,0:T(8,128)(2,1)}), bf16[16,1,1,8,2,128,128]{6,5,4,3,2,1,0:T(8,128)(2,1)}) %all-gather.3.cloned.1.call-update) | async-done | bytes 8388624 | tf_op jit(solution)/shard_map/all_gather | solution.py:58
  201.9 2.5 broadcast_in_dim.36
  204.4 223.1 %while.10 = (s32[]{:T(128)}, f32[64,128,128]{2,1,0:T(8,128)}, s32[16,12]{1,0:T(8,128)S(1)}, s32[16,8,2]{1,2,0:T(2,128)S(1)}, s32[16,12]{1,0:T(8,128)S(1)}, /*ind...) while((s32[]{:T(128)}, f32[64,128,128]{2,1,0:T(8,128)}, ...), condition=%wide.region_2.5_spmd, body=%wide.region_0.4_spmd.sunk | while | flops 103419520 | bytes 16400633 | solution.py:34
  212.3 6.1 %scatter_fusion = f32[64,128,128]{2,1,0:T(8,128)} fusion(f32[64,128,128]{2,1,0:T(8,128)} %get-tuple-element.231, s32[24]{0:T(128)S(1)} %fusion.31, f32[24,128,128]{2,1,0:T(8,128)S(1)} %copy.89), kind=kCustom, calls=%fused_computation.5.clone.1 | custom fusion | flops 393216 | bytes 4718688 | tf_op jit(solution)/shard_map/while/body/eval_jaxpr/scatter-add | solution.py:24
  226.2 6.1 %scatter_fusion = f32[64,128,128]{2,1,0:T(8,128)} fusion(f32[64,128,128]{2,1,0:T(8,128)} %get-tuple-element.231, s32[24]{0:T(128)S(1)} %fusion.31, f32[24,128,128]{2,1,0:T(8,128)S(1)} %copy.89), kind=kCustom, calls=%fused_computation.5.clone.1 | custom fusion | flops 393216 | bytes 4718688 | tf_op jit(solution)/shard_map/while/body/eval_jaxpr/scatter-add | solution.py:24
  238.1 1.4 fusion.34
  240.1 6.2 %scatter_fusion = f32[64,128,128]{2,1,0:T(8,128)} fusion(f32[64,128,128]{2,1,0:T(8,128)} %get-tuple-element.231, s32[24]{0:T(128)S(1)} %fusion.31, f32[24,128,128]{2,1,0:T(8,128)S(1)} %copy.89), kind=kCustom, calls=%fused_computation.5.clone.1 | custom fusion | flops 393216 | bytes 4718688 | tf_op jit(solution)/shard_map/while/body/eval_jaxpr/scatter-add | solution.py:24
  252.1 1.4 fusion.34
  254.2 6.1 %scatter_fusion = f32[64,128,128]{2,1,0:T(8,128)} fusion(f32[64,128,128]{2,1,0:T(8,128)} %get-tuple-element.231, s32[24]{0:T(128)S(1)} %fusion.31, f32[24,128,128]{2,1,0:T(8,128)S(1)} %copy.89), kind=kCustom, calls=%fused_computation.5.clone.1 | custom fusion | flops 393216 | bytes 4718688 | tf_op jit(solution)/shard_map/while/body/eval_jaxpr/scatter-add | solution.py:24
  268.2 6.0 %scatter_fusion = f32[64,128,128]{2,1,0:T(8,128)} fusion(f32[64,128,128]{2,1,0:T(8,128)} %get-tuple-element.231, s32[24]{0:T(128)S(1)} %fusion.31, f32[24,128,128]{2,1,0:T(8,128)S(1)} %copy.89), kind=kCustom, calls=%fused_computation.5.clone.1 | custom fusion | flops 393216 | bytes 4718688 | tf_op jit(solution)/shard_map/while/body/eval_jaxpr/scatter-add | solution.py:24
  282.1 6.1 %scatter_fusion = f32[64,128,128]{2,1,0:T(8,128)} fusion(f32[64,128,128]{2,1,0:T(8,128)} %get-tuple-element.231, s32[24]{0:T(128)S(1)} %fusion.31, f32[24,128,128]{2,1,0:T(8,128)S(1)} %copy.89), kind=kCustom, calls=%fused_computation.5.clone.1 | custom fusion | flops 393216 | bytes 4718688 | tf_op jit(solution)/shard_map/while/body/eval_jaxpr/scatter-add | solution.py:24
  296.1 6.0 %scatter_fusion = f32[64,128,128]{2,1,0:T(8,128)} fusion(f32[64,128,128]{2,1,0:T(8,128)} %get-tuple-element.231, s32[24]{0:T(128)S(1)} %fusion.31, f32[24,128,128]{2,1,0:T(8,128)S(1)} %copy.89), kind=kCustom, calls=%fused_computation.5.clone.1 | custom fusion | flops 393216 | bytes 4718688 | tf_op jit(solution)/shard_map/while/body/eval_jaxpr/scatter-add | solution.py:24
  310.0 6.0 %scatter_fusion = f32[64,128,128]{2,1,0:T(8,128)} fusion(f32[64,128,128]{2,1,0:T(8,128)} %get-tuple-element.231, s32[24]{0:T(128)S(1)} %fusion.31, f32[24,128,128]{2,1,0:T(8,128)S(1)} %copy.89), kind=kCustom, calls=%fused_computation.5.clone.1 | custom fusion | flops 393216 | bytes 4718688 | tf_op jit(solution)/shard_map/while/body/eval_jaxpr/scatter-add | solution.py:24
  321.8 1.4 fusion.34
  323.9 6.0 %scatter_fusion = f32[64,128,128]{2,1,0:T(8,128)} fusion(f32[64,128,128]{2,1,0:T(8,128)} %get-tuple-element.231, s32[24]{0:T(128)S(1)} %fusion.31, f32[24,128,128]{2,1,0:T(8,128)S(1)} %copy.89), kind=kCustom, calls=%fused_computation.5.clone.1 | custom fusion | flops 393216 | bytes 4718688 | tf_op jit(solution)/shard_map/while/body/eval_jaxpr/scatter-add | solution.py:24
  337.8 6.0 %scatter_fusion = f32[64,128,128]{2,1,0:T(8,128)} fusion(f32[64,128,128]{2,1,0:T(8,128)} %get-tuple-element.231, s32[24]{0:T(128)S(1)} %fusion.31, f32[24,128,128]{2,1,0:T(8,128)S(1)} %copy.89), kind=kCustom, calls=%fused_computation.5.clone.1 | custom fusion | flops 393216 | bytes 4718688 | tf_op jit(solution)/shard_map/while/body/eval_jaxpr/scatter-add | solution.py:24
  351.7 6.0 %scatter_fusion = f32[64,128,128]{2,1,0:T(8,128)} fusion(f32[64,128,128]{2,1,0:T(8,128)} %get-tuple-element.231, s32[24]{0:T(128)S(1)} %fusion.31, f32[24,128,128]{2,1,0:T(8,128)S(1)} %copy.89), kind=kCustom, calls=%fused_computation.5.clone.1 | custom fusion | flops 393216 | bytes 4718688 | tf_op jit(solution)/shard_map/while/body/eval_jaxpr/scatter-add | solution.py:24
  365.6 6.1 %scatter_fusion = f32[64,128,128]{2,1,0:T(8,128)} fusion(f32[64,128,128]{2,1,0:T(8,128)} %get-tuple-element.231, s32[24]{0:T(128)S(1)} %fusion.31, f32[24,128,128]{2,1,0:T(8,128)S(1)} %copy.89), kind=kCustom, calls=%fused_computation.5.clone.1 | custom fusion | flops 393216 | bytes 4718688 | tf_op jit(solution)/shard_map/while/body/eval_jaxpr/scatter-add | solution.py:24
  379.6 6.1 %scatter_fusion = f32[64,128,128]{2,1,0:T(8,128)} fusion(f32[64,128,128]{2,1,0:T(8,128)} %get-tuple-element.231, s32[24]{0:T(128)S(1)} %fusion.31, f32[24,128,128]{2,1,0:T(8,128)S(1)} %copy.89), kind=kCustom, calls=%fused_computation.5.clone.1 | custom fusion | flops 393216 | bytes 4718688 | tf_op jit(solution)/shard_map/while/body/eval_jaxpr/scatter-add | solution.py:24
  393.5 6.1 %scatter_fusion = f32[64,128,128]{2,1,0:T(8,128)} fusion(f32[64,128,128]{2,1,0:T(8,128)} %get-tuple-element.231, s32[24]{0:T(128)S(1)} %fusion.31, f32[24,128,128]{2,1,0:T(8,128)S(1)} %copy.89), kind=kCustom, calls=%fused_computation.5.clone.1 | custom fusion | flops 393216 | bytes 4718688 | tf_op jit(solution)/shard_map/while/body/eval_jaxpr/scatter-add | solution.py:24
  407.5 6.0 %scatter_fusion = f32[64,128,128]{2,1,0:T(8,128)} fusion(f32[64,128,128]{2,1,0:T(8,128)} %get-tuple-element.231, s32[24]{0:T(128)S(1)} %fusion.31, f32[24,128,128]{2,1,0:T(8,128)S(1)} %copy.89), kind=kCustom, calls=%fused_computation.5.clone.1 | custom fusion | flops 393216 | bytes 4718688 | tf_op jit(solution)/shard_map/while/body/eval_jaxpr/scatter-add | solution.py:24
  421.4 6.1 %scatter_fusion = f32[64,128,128]{2,1,0:T(8,128)} fusion(f32[64,128,128]{2,1,0:T(8,128)} %get-tuple-element.231, s32[24]{0:T(128)S(1)} %fusion.31, f32[24,128,128]{2,1,0:T(8,128)S(1)} %copy.89), kind=kCustom, calls=%fused_computation.5.clone.1 | custom fusion | flops 393216 | bytes 4718688 | tf_op jit(solution)/shard_map/while/body/eval_jaxpr/scatter-add | solution.py:24
  427.5 4.0 convert_element_type.33
  431.6 51.6 %reduce-scatter.2.cloned.1.call-done = bf16[1,8,2,128,128]{4,3,2,1,0:T(8,128)(2,1)} async-done(((bf16[4,8,2,128,128]{4,3,2,1,0:T(8,128)(2,1)}), bf16[1,8,2,128,128]{4,3,2,1,0:T(8,128)(2,1)}) %reduce-scatter.2.cloned.1.call-update) | async-done | bytes 524304 | tf_op jit(solution)/shard_map/reduce_scatter | solution.py:69
  483.1 2.1 fusion.20
  (444 shorter events, 121.7 us)
Async XLA Ops:
  6.5 113.1 %all-gather.5.cloned.1.call-start = ((), (), s32[]{:S(2)}) async-start(), calls=%async_computation.2 | async-start | bytes 7077888 | tf_op jit(solution)/shard_map/all_gather | solution.py:51
  7.3 194.6 %all-gather.3.cloned.1.call-start = ((), (), s32[]{:S(2)}) async-start(), calls=%async_computation.1 | async-start | bytes 8912896 | tf_op jit(solution)/shard_map/all_gather | solution.py:58
  8.0 475.1 %reduce-scatter.2.cloned.1.call-start = ((), (), s32[]{:S(2)}) async-start(), calls=%async_computation.3 | async-start | bytes 2621440 | tf_op jit(solution)/shard_map/reduce_scatter | solution.py:69
  427.5 4.0 copy-start.1
  427.5 55.7 %copy-start = (bf16[1,1,1,8,2,128,128]{6,5,4,3,2,1,0:T(8,128)(2,1)S(1)}, bf16[1,1,1,8,2,128,128]{6,5,4,3,2,1,0:T(8,128)(2,1)}, u32[]{:S(2)}) copy-start(bf16[1,1,1,8,2,128,128]{6,5,4,3,2,1,0:T(8,128)(2,1)} %param.21) | copy-start | bytes 1572868
Sparse Core Ops, SparseCore 0:
  9.4 85.4 all-gather.4
  97.0 104.8 all-gather.2
  431.6 51.5 reduce-scatter.1
where the time goes:
time: 495 us; the launch traced here: 492 us
  waiting for transfers between devices  135 us (27%)
  other arithmetic  112 us (23%)
  blocking collectives  111 us (22%)
  local copies, waits for them, and re-layouts  78.5 us (16%)
  matrix products  39.2 us (8%)
  between operations  13.1 us (3%)
    scatter-add x16, other arithmetic, add_piece(): summed.at[target.reshape(-1)]  97.1 us
    all_gather x1, waiting for transfers between devices, body(): lax.all_gather(x_blocks, 'row', axis=0, tiled=True)  82.3 us
    reduce_scatter x1, waiting for transfers between devices, body(): lax.psum_scatter(rounded.astype(jnp.bfloat16), 'depth', scatter_dimension...  51.6 us
    all_gather x1, blocking collectives, body(): lax.all_gather(x_cols, 'row', axis=0, tiled=True)  29.6 us
    dot_general x16, matrix products, add_piece(): jnp.einsum('akl,avlm->avkm', blocks, chosen, preferred_element_type=jnp.f...  22.6 us
    all_gather x1, blocking collectives, body(): lax.all_gather(x_flags, 'row', axis=0, tiled=True)  20.1 us
    squeeze x64, local copies, waits for them, and re-layouts, run_pieces(): summed, _ = lax.scan(one_piece, summed, (ham_part, iter_part))  20.1 us
    dot_general x16, matrix products, add_piece(): jnp.einsum('awv,awkm->avkm', paired.astype(jnp.bfloat16), picked, preferr...  16.7 us
  transfers between devices with their start and end apart: 3, of which 2 were waited for; matrix products, arithmetic and copies ran while one was open for 0% of the time, Pallas kernels for 0%

commit v1 on v0

--- a/solution.py
+++ b/solution.py
@@ -55,7 +55,9 @@
     )
     ham_all = tuple((member[0, :, 0] for member in ham_all))
     pieces = (
-        lax.all_gather(x_blocks, "row", axis=0, tiled=True),
+        jnp.concatenate(
+            lax.all_to_all(jnp.stack([x_blocks] * lax.axis_size("row")), "row", 0, 0), axis=0
+        ),
         lax.all_gather(x_cols, "row", axis=0, tiled=True),
         lax.all_gather(x_flags, "row", axis=0, tiled=True),
     )

time: 495 us -> 737 us (1.49)
  blocking collectives: 111 us -> 399 us
  waiting for transfers between devices: 135 us -> 66.2 us
  starting transfers between devices: 0.08 us -> 16 us
    all_gather x1, blocking collectives: 29.6 us -> 320 us  [body(): lax.all_gather(x_cols, 'row', axis=0, tiled=True)]
    all_gather x1 -> x0, waiting for transfers between devices: 82.3 us -> none  [body(): lax.all_gather(x_blocks, 'row', axis=0, tiled=True)]
    all_to_all x0 -> x1, starting transfers between devices: none -> 15.9 us  [body(): lax.all_to_all(jnp.stack([x_blocks] * lax.axis_size('row')), 'row', 0, 0)]
    reduce_scatter x1, waiting for transfers between devices: 51.6 us -> 65.5 us  [body(): lax.psum_scatter(rounded.astype(jnp.bfloat16), 'depth', scatter_dimension...]
  transfers between devices with their start and end apart: 3 -> 3, of which waited for: 2 -> 1; matrix products, arithmetic and copies ran while one was open for 0% -> 0% of each run, Pallas kernels for 0% -> 0%
where the time goes in v1:
time: 737 us; the launch traced here: 733 us
  blocking collectives  399 us (54%)
  other arithmetic  112 us (15%)
  local copies, waits for them, and re-layouts  84.9 us (12%)
  waiting for transfers between devices  66.2 us (9%)
  matrix products  39.2 us (5%)
  starting transfers between devices  16 us (2%)
  between operations  13.5 us (2%)
    all_gather x1, blocking collectives, body(): lax.all_gather(x_cols, 'row', axis=0, tiled=True)  320 us
    scatter-add x16, other arithmetic, add_piece(): summed.at[target.reshape(-1)]  96.6 us
    reduce_scatter x1, waiting for transfers between devices, body(): lax.psum_scatter(rounded.astype(jnp.bfloat16), 'depth', scatter_dimension...  65.5 us
    dot_general x16, matrix products, add_piece(): jnp.einsum('akl,avlm->avkm', blocks, chosen, preferred_element_type=jnp.f...  22.6 us
    all_gather x1, blocking collectives, body(): lax.all_gather(x_flags, 'row', axis=0, tiled=True)  20.4 us
    squeeze x64, local copies, waits for them, and re-layouts, run_pieces(): summed, _ = lax.scan(one_piece, summed, (ham_part, iter_part))  20.1 us
    all_gather x1, blocking collectives, body(): lax.all_gather(h_rows, 'col', axis=1, tiled=True)  16.9 us
    dot_general x16, matrix products, add_piece(): jnp.einsum('awv,awkm->avkm', paired.astype(jnp.bfloat16), picked, preferr...  16.7 us
  transfers between devices with their start and end apart: 3, of which 1 were waited for; matrix products, arithmetic and copies ran while one was open for 0% of the time, Pallas kernels for 0%

profile of v1, /device:TPU:1, one launch (start us, length us, event | category | flops | bytes accessed | tf_op | source)
XLA Modules:
  0.0 732.6 jit_solution(10654890038585790089)
XLA Ops:
  6.5 6.4 stack.2
  13.0 15.9 %all-to-all-start = ((bf16[16,1,1,1,8,2,128,128]{7,6,5,4,3,2,1,0:T(8,128)(2,1)}), bf16[16,1,1,1,8,2,128,128]{7,6,5,4,3,2,1,0:T(8,128)(2,1)}, u32[]{:S(2)}, u32[]{:S(2)}) async-start(bf16[16,1,1,1,8,2,128,128]{7,6,5,4,3,2,1,0:T(8,128)(2,1)} %stack.2), calls=%async_computation | async-start | bytes 16777216 | tf_op jit(solution)/shard_map/all_to_all | solution.py:59
  29.7 7.3 %all_gather.27 = s32[1,4,1,8,2]{3,4,2,0,1:T(2,128)S(1)} all-gather(s32[1,1,1,8,2]{3,4,2,0,1:T(2,128)S(1)} %bitcast.96), channel_id=1, replica_groups=mesh['row'=16,'col'=8,'depth'=4] {'depth'}, dimensions={1}, use_global_device_ids=true | all-gather | bytes 320 | tf_op jit(solution)/shard_map/all_gather | solution.py:40
  37.2 6.6 all_gather.29
  43.8 16.9 %all_gather.24 = s32[1,16,1,12]{3,2,0,1:T(1,128)S(1)} all-gather(s32[1,2,1,12]{3,2,0,1:T(1,128)S(1)} %bitcast.97), channel_id=1, replica_groups=mesh['row'=16,'col'=8,'depth'=4] {'col'}, dimensions={1}, use_global_device_ids=true | all-gather | bytes 864 | tf_op jit(solution)/shard_map/all_gather | solution.py:52
  60.7 13.2 %all_gather.26 = s32[1,16,1,12]{3,2,0,1:T(1,128)S(1)} all-gather(s32[1,2,1,12]{3,2,0,1:T(1,128)S(1)} %bitcast.98), channel_id=1, replica_groups=mesh['row'=16,'col'=8,'depth'=4] {'col'}, dimensions={1}, use_global_device_ids=true | all-gather | bytes 864 | tf_op jit(solution)/shard_map/all_gather | solution.py:53
  73.9 14.7 %all_gather.30 = s32[1,16,1,12]{3,2,0,1:T(1,128)S(1)} all-gather(s32[1,2,1,12]{3,2,0,1:T(1,128)S(1)} %bitcast.99), channel_id=1, replica_groups=mesh['row'=16,'col'=8,'depth'=4] {'col'}, dimensions={1}, use_global_device_ids=true | all-gather | bytes 864 | tf_op jit(solution)/shard_map/all_gather | solution.py:54
  88.6 320.1 %all_gather.25 = s32[16,1,1,8,2]{3,4,2,1,0:T(2,128)S(1)} all-gather(s32[1,1,1,8,2]{3,4,2,1,0:T(2,128)S(1)} %copy-done.2), channel_id=1, replica_groups=mesh['row'=16,'col'=8,'depth'=4] {'row'}, dimensions={0}, use_global_device_ids=true | all-gather | bytes 1088 | tf_op jit(solution)/shard_map/all_gather | solution.py:61
  408.7 20.4 %all_gather.28 = s32[16,1,1,8,2]{3,4,2,1,0:T(2,128)S(1)} all-gather(s32[1,1,1,8,2]{3,4,2,1,0:T(2,128)S(1)} %copy-done.1), channel_id=1, replica_groups=mesh['row'=16,'col'=8,'depth'=4] {'row'}, dimensions={0}, use_global_device_ids=true | all-gather | bytes 1088 | tf_op jit(solution)/shard_map/all_gather | solution.py:62
  429.1 2.5 broadcast_in_dim.36
  431.6 222.6 %while.10 = (s32[]{:T(128)}, f32[64,128,128]{2,1,0:T(8,128)}, s32[16,12]{1,0:T(8,128)S(1)}, s32[16,8,2]{1,2,0:T(2,128)S(1)}, s32[16,12]{1,0:T(8,128)S(1)}, /*ind...) while((s32[]{:T(128)}, f32[64,128,128]{2,1,0:T(8,128)}, ...), condition=%wide.region_2.5_spmd, body=%wide.region_0.4_spmd.sunk | while | flops 103419520 | bytes 16400633 | solution.py:34
  437.4 1.4 fusion.34
  439.4 5.9 scatter_fusion
  453.3 6.0 scatter_fusion
  467.2 6.1 scatter_fusion
  481.1 6.1 scatter_fusion
  495.1 6.1 scatter_fusion
  509.1 6.1 scatter_fusion
  523.0 6.0 scatter_fusion
  536.9 6.0 scatter_fusion
  550.8 6.0 scatter_fusion
  564.7 6.0 scatter_fusion
  578.5 6.0 scatter_fusion
  592.4 6.0 scatter_fusion
  604.3 1.4 fusion.34
  606.4 6.0 scatter_fusion
  620.2 6.0 scatter_fusion
  634.2 6.1 scatter_fusion
  648.1 6.0 scatter_fusion
  654.1 4.0 convert_element_type.33
  658.2 65.5 %reduce-scatter.2.cloned.1.call-done = bf16[1,8,2,128,128]{4,3,2,1,0:T(8,128)(2,1)} async-done(((bf16[4,8,2,128,128]{4,3,2,1,0:T(8,128)(2,1)}), bf16[1,8,2,128,128]{4,3,2,1,0:T(8,128)(2,1)}) %reduce-scatter.2.cloned.1.call-update) | async-done | bytes 524304 | tf_op jit(solution)/shard_map/reduce_scatter | solution.py:71
  723.7 2.1 fusion.20
  (452 shorter events, 122.4 us)
Async XLA Ops:
  13.0 16.8 %copy-start.2 = (s32[1,1,1,8,2]{3,4,2,1,0:T(2,128)S(1)}, s32[1,1,1,8,2]{3,4,2,1,0:T(2,128)}, u32[]{:S(2)}) copy-start(s32[1,1,1,8,2]{3,4,2,1,0:T(2,128)} %param.19) | copy-start | bytes 196
  13.0 24.2 %copy-start.1 = (s32[1,1,1,8,2]{3,4,2,1,0:T(2,128)S(1)}, s32[1,1,1,8,2]{3,4,2,1,0:T(2,128)}, u32[]{:S(2)}) copy-start(s32[1,1,1,8,2]{3,4,2,1,0:T(2,128)} %param.20) | copy-start | bytes 196
  13.0 30.9 %copy-start.3 = (s32[1,2,1,12]{3,2,1,0:T(1,128)S(1)}, s32[1,2,1,12]{3,2,1,0:T(1,128)}, u32[]{:S(2)}) copy-start(s32[1,2,1,12]{3,2,1,0:T(1,128)} %param.15) | copy-start | bytes 292
  13.0 47.7 %copy-start.4 = (s32[1,2,1,12]{3,2,1,0:T(1,128)S(1)}, s32[1,2,1,12]{3,2,1,0:T(1,128)}, u32[]{:S(2)}) copy-start(s32[1,2,1,12]{3,2,1,0:T(1,128)} %param.16) | copy-start | bytes 292
  13.0 60.9 %copy-start.5 = (s32[1,2,1,12]{3,2,1,0:T(1,128)S(1)}, s32[1,2,1,12]{3,2,1,0:T(1,128)}, u32[]{:S(2)}) copy-start(s32[1,2,1,12]{3,2,1,0:T(1,128)} %param.17) | copy-start | bytes 292
  13.0 416.1 %all-to-all-start = ((bf16[16,1,1,1,8,2,128,128]{7,6,5,4,3,2,1,0:T(8,128)(2,1)}), bf16[16,1,1,1,8,2,128,128]{7,6,5,4,3,2,1,0:T(8,128)(2,1)}, u32[]{:S(2)}, u32[]{:S(2)}) async-start(bf16[16,1,1,1,8,2,128,128]{7,6,5,4,3,2,1,0:T(8,128)(2,1)} %stack.2), calls=%async_computation | async-start | bytes 16777216 | tf_op jit(solution)/shard_map/all_to_all | solution.py:59
  28.9 400.2 %all-gather.2.cloned.1.call-start = ((), (), s32[]{:S(2)}) async-start(), calls=%async_computation.2 | async-start | bytes 7077888 | tf_op jit(solution)/shard_map/all_gather | solution.py:51
  29.7 694.1 %reduce-scatter.2.cloned.1.call-start = ((), (), s32[]{:S(2)}) async-start(), calls=%async_computation.3 | async-start | bytes 2621440 | tf_op jit(solution)/shard_map/reduce_scatter | solution.py:71
  654.1 69.6 %copy-start = (bf16[1,1,1,8,2,128,128]{6,5,4,3,2,1,0:T(8,128)(2,1)S(1)}, bf16[1,1,1,8,2,128,128]{6,5,4,3,2,1,0:T(8,128)(2,1)}, u32[]{:S(2)}) copy-start(bf16[1,1,1,8,2,128,128]{6,5,4,3,2,1,0:T(8,128)(2,1)} %param.21) | copy-start | bytes 1572868
Sparse Core Ops, SparseCore 0:
  31.8 81.7 all-gather.1
  658.2 65.4 reduce-scatter.1
